TPU v7x, 512 devices: a whole 4x8x8 slice. The times are simulated.
512 devices in a mesh: req: 64 (over x, z, core), tp: 8 (over y).
Axes of the slice: x: 4, y: 8, z: 8, core: 2. Of those that a mesh axis runs over, the one named last changes fastest.
Arguments:
- queries: bfloat16 [4, 512, 1024], P(None, 'req', 'tp'), may hold values from -6 to 6
- new_kv: bfloat16 [4, 512, 2, 1024], P(None, 'req', None, 'tp'), may hold values from -4 to 4
- residual: bfloat16 [4, 512, 2048], P(None, 'req'), may hold values from -1.1953125 to 1.1953125
- home_cache: bfloat16 [256, 128, 2, 1024], P('req', None, None, 'tp'), may hold values from -6 to 6
- prompt_cache: bfloat16 [256, 128, 2, 1024], P('req', None, None, 'tp'), may hold values from -6 to 6
- home_table: int32 [512, 4], P('req'), may hold values from 0 to 3
- home_len: int32 [512], P('req'), may hold values from 1 to 512, as said below
- parents: int32 [4, 512], P(None, 'req'), may hold values from 0 to 7
- prompt_place: int32 [64], P('req'), may hold values from 0 to 63, as said below
- owned_request: int32 [64], P('req'), may hold values from 0 to 63, as said below
- prompt_len: int32 [64], P('req'), may hold values from 1 to 512, as said below
- out_weight: bfloat16 [1024, 2048], P('tp'), may hold values from -0.1875 to 0.1875
- norm_gain: bfloat16 [2048], replicated, may hold values from 0.099609375 to 1.8984375
- qkv_weight: bfloat16 [2048, 3, 1024], P(None, None, 'tp'), may hold values from -0.03125 to 0.03125
Outputs:
- next_qkv: bfloat16 [4, 512, 3, 1024], P(None, 'req', None, 'tp')
- new_residual: bfloat16 [4, 512, 2048], P(None, 'req')
Inputs may be any that keep to these rules, and one draw needn't show every extreme that they name: `home_len`: some beam has all 512 tokens. `prompt_len`: some prompt has all 512 tokens. `prompt_place`: A permutation. Slot j lies on device j. The 1 request of one device have their prompts on 1 different devices, each device holds prompts of 1 request of different devices, and a request's position among its device's requests equals its slot's position j % 1. `owned_request`: the inverse permutation of prompt_place.
All inputs are finite; a program needn't handle non-finite values.
Results may differ from a plain program's by a relative error of at most 0.013.
Values may be sent and summed in bfloat16 or wider, within the bound.
No kernel may reach another device: no remote copies, remote signals or barrier semaphores. Data moves between devices by JAX's collectives and lax.ppermute only.
A program may use at most 64 MiB of HBM per device.

v0:
```python
import math
import jax
import jax.numpy as jnp
from jax import lax
from jax.sharding import PartitionSpec as P

HEAD_DIM = 64
BEAMS = 8
NEG_FILL = -1e30
NORM_EPS = 1e-05


def shards(
    queries,
    new_kv,
    residual,
    home_cache,
    prompt_cache,
    home_table,
    home_len,
    parents,
    prompt_place,
    owned_request,
    prompt_len,
    out_weight,
    norm_gain,
    qkv_weight,
):
    step_count, row_count, lane_count = queries.shape
    head_count = lane_count // HEAD_DIM
    request_count = row_count // BEAMS
    block_count = home_table.shape[1]
    block_size = home_cache.shape[1]
    prompt_tokens = prompt_cache.shape[0] * block_size // request_count
    home_tokens = block_count * block_size
    req_size = lax.axis_size("req")
    score_scale = 1.0 / math.sqrt(HEAD_DIM)
    request_base = jnp.arange(row_count, dtype=jnp.int32) // BEAMS * BEAMS
    first_parent = request_base + parents[0]
    tables = home_table[first_parent]
    lengths = home_len[first_parent]
    window = jnp.zeros((row_count, step_count, 2, lane_count), jnp.bfloat16)
    prompt_heads = prompt_cache.reshape(request_count, prompt_tokens, 2, head_count, HEAD_DIM)
    prompt_pos = jnp.arange(prompt_tokens, dtype=jnp.int32)
    home_pos = jnp.arange(home_tokens, dtype=jnp.int32)
    window_pos = jnp.arange(step_count, dtype=jnp.int32)
    gain_row = norm_gain.astype(jnp.float32)
    weight_flat = qkv_weight.reshape(qkv_weight.shape[0], 3 * lane_count)
    qkv_list = []
    residual_list = []
    for step_index in range(step_count):
        if step_index > 0:
            window = window.at[:, step_index - 1].set(new_kv[step_index - 1])
            chosen = request_base + parents[step_index]
            window = window[chosen]
            tables = tables[chosen]
            lengths = lengths[chosen]
        query_block = queries[step_index : step_index + 1]
        route_block_steps = query_block.shape[0]
        all_queries = lax.all_gather(query_block, "req", axis=1, tiled=True)
        route_query_held = all_queries.reshape(
            route_block_steps, req_size * request_count, BEAMS, head_count, HEAD_DIM
        )[:, owned_request]
        prompt_block_steps = route_query_held.shape[0]
        scores = (
            jnp.einsum(
                "krbhd,rthd->krbht",
                route_query_held,
                prompt_heads[:, :, 0],
                preferred_element_type=jnp.float32,
            )
            * score_scale
        )
        scores = jnp.where(
            prompt_pos[None, None, None, None, :] < prompt_len[None, :, None, None, None],
            scores,
            NEG_FILL,
        )
        row_top = jnp.max(scores, axis=-1)
        weights = jnp.exp(scores - row_top[..., None]).astype(jnp.bfloat16)
        weight_sum = jnp.sum(weights.astype(jnp.float32), axis=-1)
        numerator = jnp.einsum(
            "krbht,rthd->krbhd", weights, prompt_heads[:, :, 1], preferred_element_type=jnp.float32
        )
        held_numer = numerator.reshape(prompt_block_steps, row_count, lane_count)
        held_top = row_top.reshape(prompt_block_steps, row_count, head_count)
        held_sum = weight_sum.reshape(prompt_block_steps, row_count, head_count)
        all_numer = lax.all_gather(held_numer, "req", axis=1, tiled=True)
        all_top = lax.all_gather(held_top, "req", axis=1, tiled=True)
        all_sum_rows = lax.all_gather(held_sum, "req", axis=1, tiled=True)
        route_prompt_numer = all_numer.reshape(
            route_block_steps, req_size * request_count, BEAMS, lane_count
        )[:, prompt_place].reshape(route_block_steps, row_count, lane_count)
        route_prompt_top = all_top.reshape(
            route_block_steps, req_size * request_count, BEAMS, head_count
        )[:, prompt_place].reshape(route_block_steps, row_count, head_count)
        route_prompt_sum = all_sum_rows.reshape(
            route_block_steps, req_size * request_count, BEAMS, head_count
        )[:, prompt_place].reshape(route_block_steps, row_count, head_count)
        attend_prompt_numer = route_prompt_numer[0]
        attend_prompt_top = route_prompt_top[0]
        attend_prompt_sum = route_prompt_sum[0]
        query_heads = queries[step_index].reshape(row_count, head_count, HEAD_DIM)
        gathered = home_cache[tables].reshape(row_count, home_tokens, 2, head_count, HEAD_DIM)
        window_heads = window.reshape(row_count, step_count, 2, head_count, HEAD_DIM)
        own_heads = new_kv[step_index].reshape(row_count, 2, head_count, HEAD_DIM)
        home_scores = (
            jnp.einsum(
                "bhd,bthd->bht", query_heads, gathered[:, :, 0], preferred_element_type=jnp.float32
            )
            * score_scale
        )
        home_scores = jnp.where(
            home_pos[None, None, :] < lengths[:, None, None], home_scores, NEG_FILL
        )
        window_scores = (
            jnp.einsum(
                "bhd,bthd->bht",
                query_heads,
                window_heads[:, :, 0],
                preferred_element_type=jnp.float32,
            )
            * score_scale
        )
        window_scores = jnp.where(window_pos < step_index, window_scores, NEG_FILL)
        own_scores = (
            jnp.einsum(
                "bhd,bhd->bh", query_heads, own_heads[:, 0], preferred_element_type=jnp.float32
            )
            * score_scale
        )
        home_top = jnp.maximum(
            jnp.maximum(jnp.max(home_scores, axis=-1), jnp.max(window_scores, axis=-1)), own_scores
        )
        home_weights = jnp.exp(home_scores - home_top[..., None]).astype(jnp.bfloat16)
        window_weights = jnp.exp(window_scores - home_top[..., None]).astype(jnp.bfloat16)
        own_weights = jnp.exp(own_scores - home_top).astype(jnp.bfloat16)
        home_sum = (
            jnp.sum(home_weights.astype(jnp.float32), axis=-1)
            + jnp.sum(window_weights.astype(jnp.float32), axis=-1)
            + own_weights.astype(jnp.float32)
        )
        home_numer = jnp.einsum(
            "bht,bthd->bhd", home_weights, gathered[:, :, 1], preferred_element_type=jnp.float32
        )
        home_numer = home_numer + jnp.einsum(
            "bht,bthd->bhd",
            window_weights,
            window_heads[:, :, 1],
            preferred_element_type=jnp.float32,
        )
        home_numer = home_numer + own_weights.astype(jnp.float32)[..., None] * own_heads[
            :, 1
        ].astype(jnp.float32)
        attend_prompt_numer = attend_prompt_numer.reshape(row_count, head_count, HEAD_DIM)
        joint_top = jnp.maximum(home_top, attend_prompt_top)
        home_factor = jnp.exp(home_top - joint_top)
        prompt_factor = jnp.exp(attend_prompt_top - joint_top)
        joint_sum = home_sum * home_factor + attend_prompt_sum * prompt_factor
        joint_numer = (
            home_numer * home_factor[..., None] + attend_prompt_numer * prompt_factor[..., None]
        )
        attended = (
            (joint_numer / joint_sum[..., None]).astype(jnp.bfloat16).reshape(row_count, lane_count)
        )
        attended_block = attended[None]
        residual_block = residual[step_index : step_index + 1]
        block_steps = attended_block.shape[0]
        flat_rows = block_steps * row_count
        attended_flat = attended_block.reshape(flat_rows, lane_count)
        residual_flat = residual_block.reshape(flat_rows, residual_block.shape[-1])
        projected = jnp.dot(attended_flat, out_weight, preferred_element_type=jnp.float32)
        head_total = lax.psum(projected, "tp")
        mixed_rows = residual_flat.astype(jnp.float32) + head_total
        mean_square = jnp.mean(mixed_rows * mixed_rows, axis=-1, keepdims=True)
        normed = (mixed_rows * lax.rsqrt(mean_square + NORM_EPS) * gain_row).astype(jnp.bfloat16)
        residual_out = mixed_rows.astype(jnp.bfloat16)
        next_rows = jnp.dot(normed, weight_flat, preferred_element_type=jnp.float32).astype(
            jnp.bfloat16
        )
        qkv_step = next_rows.reshape(block_steps, row_count, 3, lane_count)
        residual_step = residual_out.reshape(block_steps, row_count, residual_out.shape[-1])
        qkv_list.append(qkv_step[0])
        residual_list.append(residual_step[0])
    return (jnp.stack(qkv_list), jnp.stack(residual_list))


def solution(mesh):
    placed = (
        P(None, "req", "tp"),
        P(None, "req", None, "tp"),
        P(None, "req", None),
        P("req", None, None, "tp"),
        P("req", None, None, "tp"),
        P("req", None),
        P("req"),
        P(None, "req"),
        P("req"),
        P("req"),
        P("req"),
        P("tp", None),
        P(),
        P(None, None, "tp"),
    )
    return jax.shard_map(
        shards,
        mesh=mesh,
        in_specs=placed,
        out_specs=(P(None, "req", None, "tp"), P(None, "req", None)),
        check_vma=False,
    )
```

profile of v0, /device:TPU:2, one launch (start us, length us, event | category | flops | bytes accessed | tf_op | source)
XLA Modules:
  0.0 910.0 jit_solution(6705653716037907314)
XLA Ops:
  7.2 0.8 fusion.152
  8.2 0.8 fusion.133
  9.0 0.8 copy.148
  12.4 6.4 gather_fusion.9
  18.8 2.8 copy.172
  21.6 3.1 reshape.675
  24.7 1.4 slice_bitcast_fusion.3
  30.8 1.9 fusion.22
  33.4 1.3 convert_reduce_fusion.3
  34.7 1.2 convert_reduce_fusion.9
  35.9 55.4 %all_gather.56 = bf16[1,512,128]{2,1,0:T(8,128)(2,1)S(1)} all-gather(bf16[1,8,128]{2,1,0:T(8,128)(2,1)S(1)} %get-tuple-element.276), channel_id=1, replica_groups=mesh['req'=64,'tp'=8] {'req'}, dimensions={1}, use_global_device_ids=true | all-gather | bytes 133120 | tf_op jit(solution)/shard_map/all_gather | solution.py:60
  92.8 48.2 %all_gather.60 = bf16[1,512,128]{2,1,0:T(8,128)(2,1)S(1)} all-gather(bf16[1,8,128]{2,1,0:T(8,128)(2,1)S(1)} %get-tuple-element.279), channel_id=1, replica_groups=mesh['req'=64,'tp'=8] {'req'}, dimensions={1}, use_global_device_ids=true | all-gather | bytes 133120 | tf_op jit(solution)/shard_map/all_gather | solution.py:60
  142.4 0.7 convert_reduce_fusion.2
  143.2 0.8 convolution_bitcast_fusion.1
  145.0 5.4 gather_fusion.13
  150.4 2.8 copy.181
  153.2 3.1 reshape.687
  156.3 1.4 slice_bitcast_fusion.1
  159.1 1.9 fusion.18
  161.7 1.3 convert_reduce_fusion.1
  162.9 1.2 convert_reduce_fusion.8
  164.4 0.7 convert_reduce_fusion
  165.1 0.8 convolution_bitcast_fusion
  167.7 5.4 gather_fusion.5
  173.1 2.8 copy.163
  175.9 3.1 reshape.663
  179.0 1.2 slice_bitcast_fusion.5
  181.6 1.3 convert_reduce_fusion.5
  182.8 1.2 convert_reduce_fusion.10
  184.1 48.3 %all_gather.52 = bf16[1,512,128]{2,1,0:T(8,128)(2,1)S(1)} all-gather(bf16[1,8,128]{2,1,0:T(8,128)(2,1)S(1)} %get-tuple-element.277), channel_id=1, replica_groups=mesh['req'=64,'tp'=8] {'req'}, dimensions={1}, use_global_device_ids=true | all-gather | bytes 133120 | tf_op jit(solution)/shard_map/all_gather | solution.py:60
  232.3 47.7 %all_gather.48 = bf16[1,512,128]{2,1,0:T(8,128)(2,1)S(1)} all-gather(bf16[1,8,128]{2,1,0:T(8,128)(2,1)S(1)} %get-tuple-element.278), channel_id=1, replica_groups=mesh['req'=64,'tp'=8] {'req'}, dimensions={1}, use_global_device_ids=true | all-gather | bytes 133120 | tf_op jit(solution)/shard_map/all_gather | solution.py:60
  280.1 0.9 reshape.650
  281.1 0.7 constant_dynamic-slice_fusion.11
  281.8 0.9 fusion.154
  283.3 0.9 fusion.153
  284.6 42.4 %all-gather.13 = f32[64,8,2]{1,2,0:T(2,128)S(1)} all-gather(f32[1,8,2]{1,2,0:T(2,128)} %bitcast.533), channel_id=7, replica_groups=mesh['req'=64,'tp'=8] {'req'}, dimensions={0}, use_global_device_ids=true | all-gather | bytes 4160 | tf_op jit(solution)/shard_map/all_gather | solution.py:90
  327.0 41.3 %all-gather.12 = f32[64,8,2]{1,2,0:T(2,128)S(1)} all-gather(f32[1,8,2]{1,2,0:T(2,128)S(1)} %bitcast.517), channel_id=6, replica_groups=mesh['req'=64,'tp'=8] {'req'}, dimensions={0}, use_global_device_ids=true | all-gather | bytes 4160 | tf_op jit(solution)/shard_map/all_gather | solution.py:89
  369.3 0.8 copy.228
  370.9 43.2 %all_gather.58 = f32[1,512,128]{2,1,0:T(8,128)S(1)} all-gather(f32[1,8,128]{2,1,0:T(8,128)S(1)} %reshape.683), channel_id=1, replica_groups=mesh['req'=64,'tp'=8] {'req'}, dimensions={1}, use_global_device_ids=true | all-gather | bytes 266240 | tf_op jit(solution)/shard_map/all_gather | solution.py:88
  414.2 1.4 fusion.20
  415.8 0.9 fusion.90
  416.7 41.3 %all-gather.15 = f32[64,8,2]{1,2,0:T(2,128)S(1)} all-gather(f32[1,8,2]{1,2,0:T(2,128)} %bitcast.534), channel_id=9, replica_groups=mesh['req'=64,'tp'=8] {'req'}, dimensions={0}, use_global_device_ids=true | all-gather | bytes 4160 | tf_op jit(solution)/shard_map/all_gather | solution.py:90
  458.0 42.8 %all-gather.14 = f32[64,8,2]{1,2,0:T(2,128)S(1)} all-gather(f32[1,8,2]{1,2,0:T(2,128)} %bitcast.518), channel_id=8, replica_groups=mesh['req'=64,'tp'=8] {'req'}, dimensions={0}, use_global_device_ids=true | all-gather | bytes 4160 | tf_op jit(solution)/shard_map/all_gather | solution.py:89
  501.9 0.8 copy.243
  503.4 41.7 %all_gather.62 = f32[1,512,128]{2,1,0:T(8,128)S(1)} all-gather(f32[1,8,128]{2,1,0:T(8,128)S(1)} %reshape.695), channel_id=1, replica_groups=mesh['req'=64,'tp'=8] {'req'}, dimensions={1}, use_global_device_ids=true | all-gather | bytes 266240 | tf_op jit(solution)/shard_map/all_gather | solution.py:88
  546.3 0.8 fusion.159
  547.1 0.8 fusion.160
  547.9 42.8 %all-gather.11 = f32[64,8,2]{1,2,0:T(2,128)S(1)} all-gather(f32[1,8,2]{1,2,0:T(2,128)S(1)} %bitcast.535), channel_id=5, replica_groups=mesh['req'=64,'tp'=8] {'req'}, dimensions={0}, use_global_device_ids=true | all-gather | bytes 4160 | tf_op jit(solution)/shard_map/all_gather | solution.py:90
  590.7 41.3 %all-gather.10 = f32[64,8,2]{1,2,0:T(2,128)S(1)} all-gather(f32[1,8,2]{1,2,0:T(2,128)S(1)} %bitcast.519), channel_id=4, replica_groups=mesh['req'=64,'tp'=8] {'req'}, dimensions={0}, use_global_device_ids=true | all-gather | bytes 4160 | tf_op jit(solution)/shard_map/all_gather | solution.py:89
  632.6 43.4 %all_gather.54 = f32[1,512,128]{2,1,0:T(8,128)S(1)} all-gather(f32[1,8,128]{2,1,0:T(8,128)S(1)} %reshape.671), channel_id=1, replica_groups=mesh['req'=64,'tp'=8] {'req'}, dimensions={1}, use_global_device_ids=true | all-gather | bytes 266240 | tf_op jit(solution)/shard_map/all_gather | solution.py:88
  677.1 0.8 fusion.158
  678.1 5.4 gather_fusion.2
  683.5 2.8 copy.151
  686.3 3.1 reshape.649
  689.4 1.5 slice_bitcast_fusion.7
  691.2 1.9 fusion.30
  693.4 41.3 %all-gather.9 = f32[64,8,2]{1,2,0:T(2,128)S(1)} all-gather(f32[1,8,2]{1,2,0:T(2,128)S(1)} %bitcast.532), channel_id=3, replica_groups=mesh['req'=64,'tp'=8] {'req'}, dimensions={0}, use_global_device_ids=true | all-gather | bytes 4160 | tf_op jit(solution)/shard_map/all_gather | solution.py:90
  734.7 42.8 %all-gather.8 = f32[64,8,2]{1,2,0:T(2,128)S(1)} all-gather(f32[1,8,2]{1,2,0:T(2,128)S(1)} %bitcast.516), channel_id=2, replica_groups=mesh['req'=64,'tp'=8] {'req'}, dimensions={0}, use_global_device_ids=true | all-gather | bytes 4160 | tf_op jit(solution)/shard_map/all_gather | solution.py:89
  778.3 41.7 %all_gather.50 = f32[1,512,128]{2,1,0:T(8,128)S(1)} all-gather(f32[1,8,128]{2,1,0:T(8,128)S(1)} %reshape.658), channel_id=1, replica_groups=mesh['req'=64,'tp'=8] {'req'}, dimensions={1}, use_global_device_ids=true | all-gather | bytes 266240 | tf_op jit(solution)/shard_map/all_gather | solution.py:88
  820.9 0.8 fusion.157
  821.8 1.7 copy.160
  823.5 73.9 %all-reduce.4.cloned.1.call-done = (f32[8,2048]{1,0:T(8,128)}, f32[8,2048]{1,0:T(8,128)}, f32[8,2048]{1,0:T(8,128)}, f32[8,2048]{1,0:T(8,128)}) async-done(((f32[8,2048]{1,0:T(8,128)}, f32[8,2048]{1,0:T(8,128)}, f32[8,2048]{1,0:T(8,128)}, f32[8,2048]{1,0:T(8,128)}), (f32[8,2048]{1,0:T(8,128)}, f32[8,2048]{1,0:T(8,128)}, f32[8,2048]{1,0:T(8,128)}, f32[8,2048]{1,0:T(8,128)})) %all-reduce.4.cloned.1.call-update) | async-done | bytes 262160 | tf_op jit(solution)/shard_map/psum | solution.py:173
  897.5 1.1 multiply_reduce_fusion.3
  898.6 1.3 fusion.12
  (244 shorter events, 28.4 us)
Async XLA Ops:
  7.2 539.1 %copy-start = (bf16[128,2048]{1,0:T(8,128)(2,1)S(1)}, bf16[128,2048]{1,0:T(8,128)(2,1)}, u32[]{:S(2)}) copy-start(bf16[128,2048]{1,0:T(8,128)(2,1)} %param.31) | copy-start | bytes 1572868
  7.2 890.3 %all-reduce.4.cloned.1.call-start = ((), (), s32[]{:S(2)}) async-start(), calls=%async_computation | async-start | bytes 524288 | tf_op jit(solution)/shard_map/psum | solution.py:173
  24.7 1.5 copy-start.1
  24.7 3.5 copy-start.12
  26.8 114.4 %copy-start.8 = (bf16[4,128,2,128]{3,2,1,0:T(2,128)(2,1)S(1)}, bf16[4,128,2,128]{3,2,1,0:T(2,128)(2,1)}, u32[]{:S(2)}) copy-start(bf16[4,128,2,128]{3,2,1,0:T(2,128)(2,1)} %param.24) | copy-start | bytes 786436
  30.8 114.2 %copy-start.2 = (bf16[4,128,2,128]{3,2,1,0:T(2,128)(2,1)S(1)}, bf16[4,128,2,128]{3,2,1,0:T(2,128)(2,1)}, u32[]{:S(2)}) copy-start(bf16[4,128,2,128]{3,2,1,0:T(2,128)(2,1)} %param.23) | copy-start | bytes 786436
  33.0 117.4 %copy-start.13 = (bf16[8,2,2,64]{3,2,1,0:T(2,128)(2,1)}, bf16[8,2,2,64]{3,2,1,0:T(2,128)(2,1)S(1)}, u32[]{:S(2)}) copy-start(bf16[8,2,2,64]{3,2,1,0:T(2,128)(2,1)S(1)} %reshape_squeeze.29) | copy-start | bytes 12292
  33.2 109.0 %copy-start.29 = (f32[8,2]{0,1:T(2,128)}, f32[8,2]{0,1:T(2,128)S(1)}, u32[]{:S(2)}) copy-start(f32[8,2]{0,1:T(2,128)S(1)} %copy.224) | copy-start | bytes 196
  33.4 117.0 %copy-start.19 = (f32[8,2]{0,1:T(2,128)}, f32[8,2]{0,1:T(2,128)S(1)}, u32[]{:S(2)}) copy-start(f32[8,2]{0,1:T(2,128)S(1)} %maximum_maximum_fusion.1) | copy-start | bytes 196
  142.1 22.0 %copy-start.33 = (pred[512]{0:T(512)(128)(4,1)}, pred[512]{0:T(512)(128)(4,1)S(1)}, u32[]{:S(2)}) copy-start(pred[512]{0:T(512)(128)(4,1)S(1)} %iota_compare_fusion.4) | copy-start | bytes 1540
  161.3 6.4 copy-start.14
  161.5 11.7 %copy-start.30 = (f32[8,2]{0,1:T(2,128)}, f32[8,2]{0,1:T(2,128)S(1)}, u32[]{:S(2)}) copy-start(f32[8,2]{0,1:T(2,128)S(1)} %copy.239) | copy-start | bytes 196
  161.7 6.0 copy-start.20
  164.4 3.3 copy-start.18
  180.2 234.0 %copy-start.3 = (bf16[8,512,2,64]{1,0,3,2:T(8,128)(2,1)S(1)}, bf16[8,512,2,64]{1,0,3,2:T(8,128)(2,1)}, u32[]{:S(2)}) copy-start(bf16[8,512,2,64]{1,0,3,2:T(8,128)(2,1)} %get-tuple-element.246) | copy-start | bytes 3145732
  181.2 1.7 copy-start.16
  181.4 1.5 copy-start.31
  181.6 1.3 copy-start.21
  184.1 361.2 %copy-start.4 = (bf16[8,512,2,64]{1,0,3,2:T(8,128)(2,1)S(1)}, bf16[8,512,2,64]{1,0,3,2:T(8,128)(2,1)}, u32[]{:S(2)}) copy-start(bf16[8,512,2,64]{1,0,3,2:T(8,128)(2,1)} %get-tuple-element.248) | copy-start | bytes 3145732
  281.1 134.6 %copy-start.26 = (bf16[8,4,2,64]{3,2,1,0:T(2,128)(2,1)S(1)}, bf16[8,4,2,64]{3,2,1,0:T(2,128)(2,1)}, u32[]{:S(2)}) copy-start(bf16[8,4,2,64]{3,2,1,0:T(2,128)(2,1)} %get-tuple-element.265) | copy-start | bytes 24580
  281.1 264.1 %copy-start.23 = (bf16[8,2,512,1]{2,0,1,3:T(8,128)(2,1)S(1)}, bf16[8,2,512,1]{2,0,1,3:T(8,128)(2,1)}, u32[]{:S(2)}) copy-start(bf16[8,2,512,1]{2,0,1,3:T(8,128)(2,1)} %get-tuple-element.260) | copy-start | bytes 49156
  282.9 263.1 %copy-start.28 = (bf16[8,4,2,64]{3,2,1,0:T(2,128)(2,1)S(1)}, bf16[8,4,2,64]{3,2,1,0:T(2,128)(2,1)}, u32[]{:S(2)}) copy-start(bf16[8,4,2,64]{3,2,1,0:T(2,128)(2,1)} %get-tuple-element.267) | copy-start | bytes 24580
  282.9 263.2 %copy-start.15 = (bf16[8,2,2,64]{3,2,1,0:T(2,128)(2,1)S(1)}, bf16[8,2,2,64]{3,2,1,0:T(2,128)(2,1)}, u32[]{:S(2)}) copy-start(bf16[8,2,2,64]{3,2,1,0:T(2,128)(2,1)} %copy-done.14) | copy-start | bytes 12292
  414.2 217.8 %copy-start.22 = (f32[8,2]{0,1:T(2,128)S(1)}, f32[8,2]{0,1:T(2,128)}, u32[]{:S(2)}) copy-start(f32[8,2]{0,1:T(2,128)} %copy-done.21) | copy-start | bytes 196
  414.2 217.8 %copy-start.32 = (f32[8,2]{0,1:T(2,128)S(1)}, f32[8,2]{0,1:T(2,128)}, u32[]{:S(2)}) copy-start(f32[8,2]{0,1:T(2,128)} %copy-done.31) | copy-start | bytes 196
  414.2 217.8 %copy-start.36 = (f32[8,2]{0,1:T(2,128)S(1)}, f32[8,2]{0,1:T(2,128)}, u32[]{:S(2)}) copy-start(f32[8,2]{0,1:T(2,128)} %get-tuple-element.261) | copy-start | bytes 196
  414.2 217.8 %copy-start.38 = (f32[8,2]{0,1:T(2,128)S(1)}, f32[8,2]{0,1:T(2,128)}, u32[]{:S(2)}) copy-start(f32[8,2]{0,1:T(2,128)} %get-tuple-element.238) | copy-start | bytes 196
  414.2 218.1 %copy-start.34 = (bf16[8,2,4]{0,2,1:T(4,128)(2,1)S(1)}, bf16[8,2,4]{0,2,1:T(4,128)(2,1)}, u32[]{:S(2)}) copy-start(bf16[8,2,4]{0,2,1:T(4,128)(2,1)} %get-tuple-element.239) | copy-start | bytes 388
  415.6 260.5 %copy-start.5 = (bf16[8,512,2,64]{1,0,3,2:T(8,128)(2,1)S(1)}, bf16[8,512,2,64]{1,0,3,2:T(8,128)(2,1)}, u32[]{:S(2)}) copy-start(bf16[8,512,2,64]{1,0,3,2:T(8,128)(2,1)} %get-tuple-element.250) | copy-start | bytes 3145732
  415.6 260.5 %copy-start.24 = (bf16[8,2,512,1]{2,0,1,3:T(8,128)(2,1)S(1)}, bf16[8,2,512,1]{2,0,1,3:T(8,128)(2,1)}, u32[]{:S(2)}) copy-start(bf16[8,2,512,1]{2,0,1,3:T(8,128)(2,1)} %get-tuple-element.262) | copy-start | bytes 49156
  545.2 131.5 %copy-start.27 = (bf16[8,4,2,64]{3,2,0,1:T(2,128)(2,1)S(1)}, bf16[8,4,2,64]{3,2,0,1:T(2,128)(2,1)}, u32[]{:S(2)}) copy-start(bf16[8,4,2,64]{3,2,0,1:T(2,128)(2,1)} %get-tuple-element.269) | copy-start | bytes 24580
  545.2 131.7 %copy-start.17 = (bf16[8,2,2,64]{3,2,1,0:T(2,128)(2,1)S(1)}, bf16[8,2,2,64]{3,2,1,0:T(2,128)(2,1)}, u32[]{:S(2)}) copy-start(bf16[8,2,2,64]{3,2,1,0:T(2,128)(2,1)} %copy-done.16) | copy-start | bytes 12292
  545.9 132.0 %copy-start.35 = (s32[8,4,1]{0,1,2:T(4,128)S(1)}, s32[8,4,1]{0,1,2:T(4,128)}, u32[]{:S(2)}) copy-start(s32[8,4,1]{0,1,2:T(4,128)} %get-tuple-element.299) | copy-start | bytes 388
  689.4 1.5 copy-start.25
  690.9 129.2 %copy-start.6 = (bf16[8,512,2,64]{1,0,3,2:T(8,128)(2,1)S(1)}, bf16[8,512,2,64]{1,0,3,2:T(8,128)(2,1)}, u32[]{:S(2)}) copy-start(bf16[8,512,2,64]{1,0,3,2:T(8,128)(2,1)} %get-tuple-element.252) | copy-start | bytes 3145732
  820.7 2.8 copy-start.37
  820.7 76.7 %copy-start.7 = (bf16[4,8,2048]{2,1,0:T(8,128)(2,1)S(1)}, bf16[4,8,2048]{2,1,0:T(8,128)(2,1)}, u32[]{:S(2)}) copy-start(bf16[4,8,2048]{2,1,0:T(8,128)(2,1)} %param.22) | copy-start | bytes 393220
  897.5 2.5 copy-start.11
  897.5 3.1 copy-start.10
  900.0 1.1 copy-start.9
Sparse Core Ops, SparseCore 0:
  821.9 75.5 all-reduce.3
where the time goes:
time: 916 us; the launch traced here: 910 us
  blocking collectives  706 us (77%)
  local copies, waits for them, and re-layouts  74.7 us (8%)
  waiting for transfers between devices  73.9 us (8%)
  matrix products  21.2 us (2%)
  other arithmetic  17.5 us (2%)
  between operations  16.8 us (2%)
    all_gather x4, blocking collectives, shards(): all_queries = lax.all_gather(query_block, 'req', axis=1, tiled=True)  200 us
    all_gather x4, blocking collectives, shards(): all_numer = lax.all_gather(held_numer, 'req', axis=1, tiled=True)  170 us
    all_gather x4, blocking collectives, shards(): all_top = lax.all_gather(held_top, 'req', axis=1, tiled=True)  168 us
    all_gather x4, blocking collectives, shards(): all_sum_rows = lax.all_gather(held_sum, 'req', axis=1, tiled=True)  168 us
    psum x1, waiting for transfers between devices, shards(): head_total = lax.psum(projected, 'tp')  73.9 us
    gather x8, local copies, waits for them, and re-layouts, shards(): home_cache[tables].reshape(row_count, home_tokens, 2, head_count, HEAD_DIM)  33.7 us
  transfers between devices with their start and end apart: 1, of which 1 were waited for; matrix products, arithmetic and copies ran while one was open for 0% of the time, Pallas kernels for 0%

commit v1 on v0

--- a/solution.py
+++ b/solution.py
@@ -86,8 +86,13 @@
         held_top = row_top.reshape(prompt_block_steps, row_count, head_count)
         held_sum = weight_sum.reshape(prompt_block_steps, row_count, head_count)
         all_numer = lax.all_gather(held_numer, "req", axis=1, tiled=True)
-        all_top = lax.all_gather(held_top, "req", axis=1, tiled=True)
-        all_sum_rows = lax.all_gather(held_sum, "req", axis=1, tiled=True)
+        all_top, all_sum_rows = jnp.split(
+            lax.all_gather(
+                jnp.concatenate([held_top, held_sum], axis=0), "req", axis=1, tiled=True
+            ),
+            [held_top.shape[0]],
+            axis=0,
+        )
         route_prompt_numer = all_numer.reshape(
             route_block_steps, req_size * request_count, BEAMS, lane_count
         )[:, prompt_place].reshape(route_block_steps, row_count, lane_count)

time: 916 us -> 760 us (0.83)
  blocking collectives: 706 us -> 564 us
  other arithmetic: 17.5 us -> 6.92 us
    all_gather x8 -> x4, blocking collectives: 336 us -> 197 us  [shards(): lax.all_gather(jnp.concatenate([held_top, held_sum], axis=0), 'req', axis...]
where the time goes in v1:
time: 760 us; the launch traced here: 751 us
  blocking collectives  564 us (74%)
  waiting for transfers between devices  73.9 us (10%)
  local copies, waits for them, and re-layouts  70.7 us (9%)
  matrix products  19.1 us (3%)
  between operations  16.7 us (2%)
    all_gather x4, blocking collectives, shards(): all_queries = lax.all_gather(query_block, 'req', axis=1, tiled=True)  200 us
    all_gather x4, blocking collectives, shards(): lax.all_gather(jnp.concatenate([held_top, held_sum], axis=0), 'req', axis...  197 us
    all_gather x4, blocking collectives, shards(): all_numer = lax.all_gather(held_numer, 'req', axis=1, tiled=True)  167 us
    psum x1, waiting for transfers between devices, shards(): head_total = lax.psum(projected, 'tp')  73.9 us
    gather x8, local copies, waits for them, and re-layouts, shards(): home_cache[tables].reshape(row_count, home_tokens, 2, head_count, HEAD_DIM)  33.7 us
  transfers between devices with their start and end apart: 1, of which 1 were waited for; matrix products, arithmetic and copies ran while one was open for 0% of the time, Pallas kernels for 0%

profile of v1, /device:TPU:2, one launch (start us, length us, event | category | flops | bytes accessed | tf_op | source)
XLA Modules:
  0.0 751.0 jit_solution(12247263491195375339)
XLA Ops:
  7.2 0.8 fusion.140
  8.2 0.8 fusion.117
  9.0 0.8 copy.168
  9.8 0.6 gather_fusion.1
  10.4 0.6 gather_fusion.4
  10.9 0.6 gather_fusion.8
  11.6 0.6 gather_fusion.12
  12.4 6.4 gather_fusion.9
  18.8 2.8 copy.198
  21.6 3.1 reshape.675
  24.7 1.4 slice_bitcast_fusion.3
  26.1 0.6 gather_fusion
  26.8 0.6 gather_fusion.3
  27.4 0.6 gather_fusion.7
  28.2 0.6 gather_fusion.6
  28.9 0.6 gather_fusion.10
  29.6 1.9 fusion.22
  32.5 55.4 %all_gather.42 = bf16[1,512,128]{2,1,0:T(8,128)(2,1)S(1)} all-gather(bf16[1,8,128]{2,1,0:T(8,128)(2,1)S(1)} %get-tuple-element.284), channel_id=1, replica_groups=mesh['req'=64,'tp'=8] {'req'}, dimensions={1}, use_global_device_ids=true | all-gather | bytes 133120 | tf_op jit(solution)/shard_map/all_gather | solution.py:60
  89.4 47.8 %all_gather.45 = bf16[1,512,128]{2,1,0:T(8,128)(2,1)S(1)} all-gather(bf16[1,8,128]{2,1,0:T(8,128)(2,1)S(1)} %get-tuple-element.287), channel_id=1, replica_groups=mesh['req'=64,'tp'=8] {'req'}, dimensions={1}, use_global_device_ids=true | all-gather | bytes 133120 | tf_op jit(solution)/shard_map/all_gather | solution.py:60
  139.0 0.7 gather_fusion.11
  139.9 5.4 gather_fusion.13
  145.3 2.8 copy.210
  148.1 3.1 reshape.687
  151.2 1.4 slice_bitcast_fusion.1
  152.7 0.6 gather_fusion.14
  153.4 1.9 fusion.18
  157.0 48.6 %all_gather.39 = bf16[1,512,128]{2,1,0:T(8,128)(2,1)S(1)} all-gather(bf16[1,8,128]{2,1,0:T(8,128)(2,1)S(1)} %get-tuple-element.285), channel_id=1, replica_groups=mesh['req'=64,'tp'=8] {'req'}, dimensions={1}, use_global_device_ids=true | all-gather | bytes 133120 | tf_op jit(solution)/shard_map/all_gather | solution.py:60
  206.1 5.4 gather_fusion.5
  211.5 2.8 copy.186
  214.3 3.1 reshape.663
  217.4 1.1 slice_bitcast_fusion.5
  218.5 0.7 fusion.26
  220.1 47.8 %all_gather.36 = bf16[1,512,128]{2,1,0:T(8,128)(2,1)S(1)} all-gather(bf16[1,8,128]{2,1,0:T(8,128)(2,1)S(1)} %get-tuple-element.286), channel_id=1, replica_groups=mesh['req'=64,'tp'=8] {'req'}, dimensions={1}, use_global_device_ids=true | all-gather | bytes 133120 | tf_op jit(solution)/shard_map/all_gather | solution.py:60
  269.8 48.7 %all_gather.43 = f32[2,512,2]{2,0,1:T(2,128)S(1)} all-gather(f32[2,8,2]{2,0,1:T(2,128)S(1)} %copy.201), channel_id=1, replica_groups=mesh['req'=64,'tp'=8] {'req'}, dimensions={1}, use_global_device_ids=true | all-gather | bytes 8320 | tf_op jit(solution)/shard_map/all_gather | solution.py:90
  319.6 41.7 %all_gather.44 = f32[1,512,128]{2,1,0:T(8,128)S(1)} all-gather(f32[1,8,128]{2,1,0:T(8,128)S(1)} %reshape.684), channel_id=1, replica_groups=mesh['req'=64,'tp'=8] {'req'}, dimensions={1}, use_global_device_ids=true | all-gather | bytes 266240 | tf_op jit(solution)/shard_map/all_gather | solution.py:88
  361.4 0.7 fusion.20
  362.5 49.5 %all_gather.46 = f32[2,512,2]{2,0,1:T(2,128)S(1)} all-gather(f32[2,8,2]{2,0,1:T(2,128)S(1)} %copy.213), channel_id=1, replica_groups=mesh['req'=64,'tp'=8] {'req'}, dimensions={1}, use_global_device_ids=true | all-gather | bytes 8320 | tf_op jit(solution)/shard_map/all_gather | solution.py:90
  413.1 41.7 %all_gather.47 = f32[1,512,128]{2,1,0:T(8,128)S(1)} all-gather(f32[1,8,128]{2,1,0:T(8,128)S(1)} %reshape.696), channel_id=1, replica_groups=mesh['req'=64,'tp'=8] {'req'}, dimensions={1}, use_global_device_ids=true | all-gather | bytes 266240 | tf_op jit(solution)/shard_map/all_gather | solution.py:88
  454.9 0.7 fusion.16
  455.9 0.8 fusion.147
  456.7 0.8 fusion.148
  457.6 49.3 %all_gather.40 = f32[2,512,2]{2,0,1:T(2,128)S(1)} all-gather(f32[2,8,2]{2,0,1:T(2,128)S(1)} %copy.189), channel_id=1, replica_groups=mesh['req'=64,'tp'=8] {'req'}, dimensions={1}, use_global_device_ids=true | all-gather | bytes 8320 | tf_op jit(solution)/shard_map/all_gather | solution.py:90
  508.1 41.7 %all_gather.41 = f32[1,512,128]{2,1,0:T(8,128)S(1)} all-gather(f32[1,8,128]{2,1,0:T(8,128)S(1)} %reshape.672), channel_id=1, replica_groups=mesh['req'=64,'tp'=8] {'req'}, dimensions={1}, use_global_device_ids=true | all-gather | bytes 266240 | tf_op jit(solution)/shard_map/all_gather | solution.py:88
  549.9 0.7 fusion.24
  550.9 0.8 fusion.146
  551.8 49.5 %all_gather.37 = f32[2,512,2]{2,0,1:T(2,128)S(1)} all-gather(f32[2,8,2]{2,0,1:T(2,128)S(1)} %copy.176), channel_id=1, replica_groups=mesh['req'=64,'tp'=8] {'req'}, dimensions={1}, use_global_device_ids=true | all-gather | bytes 8320 | tf_op jit(solution)/shard_map/all_gather | solution.py:90
  601.3 0.4 fusion.138
  602.1 5.4 gather_fusion.2
  607.5 2.8 copy.171
  610.3 3.1 reshape.649
  613.4 1.5 slice_bitcast_fusion.7
  615.1 1.9 fusion.30
  618.0 41.7 %all_gather.38 = f32[1,512,128]{2,1,0:T(8,128)S(1)} all-gather(f32[1,8,128]{2,1,0:T(8,128)S(1)} %reshape.659), channel_id=1, replica_groups=mesh['req'=64,'tp'=8] {'req'}, dimensions={1}, use_global_device_ids=true | all-gather | bytes 266240 | tf_op jit(solution)/shard_map/all_gather | solution.py:88
  659.8 1.9 fusion.28
  661.9 0.8 fusion.145
  662.8 1.7 copy.183
  664.5 73.9 %all-reduce.4.cloned.1.call-done = (f32[8,2048]{1,0:T(8,128)}, f32[8,2048]{1,0:T(8,128)}, f32[8,2048]{1,0:T(8,128)}, f32[8,2048]{1,0:T(8,128)}) async-done(((f32[8,2048]{1,0:T(8,128)}, f32[8,2048]{1,0:T(8,128)}, f32[8,2048]{1,0:T(8,128)}, f32[8,2048]{1,0:T(8,128)}), (f32[8,2048]{1,0:T(8,128)}, f32[8,2048]{1,0:T(8,128)}, f32[8,2048]{1,0:T(8,128)}, f32[8,2048]{1,0:T(8,128)})) %all-reduce.4.cloned.1.call-update) | async-done | bytes 262160 | tf_op jit(solution)/shard_map/psum | solution.py:178
  738.5 1.1 multiply_reduce_fusion.3
  739.6 1.3 fusion.12
  741.0 0.5 fusion.13
  741.5 0.5 fusion.14
  742.1 0.5 fusion.15
  742.6 0.7 pad_maximum_fusion
  743.3 0.6 pad_maximum_fusion.1
  (216 shorter events, 15.2 us)
Async XLA Ops:
  7.2 448.8 %copy-start = (bf16[128,2048]{1,0:T(8,128)(2,1)S(1)}, bf16[128,2048]{1,0:T(8,128)(2,1)}, u32[]{:S(2)}) copy-start(bf16[128,2048]{1,0:T(8,128)(2,1)} %param.31) | copy-start | bytes 1572868
  7.2 731.3 %all-reduce.4.cloned.1.call-start = ((), (), s32[]{:S(2)}) async-start(), calls=%async_computation | async-start | bytes 524288 | tf_op jit(solution)/shard_map/psum | solution.py:178
  24.7 1.5 copy-start.1
  24.7 3.5 copy-start.11
  26.8 110.5 %copy-start.7 = (bf16[4,128,2,128]{3,2,1,0:T(2,128)(2,1)S(1)}, bf16[4,128,2,128]{3,2,1,0:T(2,128)(2,1)}, u32[]{:S(2)}) copy-start(bf16[4,128,2,128]{3,2,1,0:T(2,128)(2,1)} %param.24) | copy-start | bytes 786436
  29.6 110.3 %copy-start.2 = (bf16[4,128,2,128]{3,2,1,0:T(2,128)(2,1)S(1)}, bf16[4,128,2,128]{3,2,1,0:T(2,128)(2,1)}, u32[]{:S(2)}) copy-start(bf16[4,128,2,128]{3,2,1,0:T(2,128)(2,1)} %param.23) | copy-start | bytes 786436
  219.2 142.2 %copy-start.3 = (bf16[8,512,2,64]{1,0,3,2:T(8,128)(2,1)S(1)}, bf16[8,512,2,64]{1,0,3,2:T(8,128)(2,1)}, u32[]{:S(2)}) copy-start(bf16[8,512,2,64]{1,0,3,2:T(8,128)(2,1)} %get-tuple-element.246) | copy-start | bytes 3145732
  318.9 136.0 %copy-start.4 = (bf16[8,512,2,64]{1,0,3,2:T(8,128)(2,1)S(1)}, bf16[8,512,2,64]{1,0,3,2:T(8,128)(2,1)}, u32[]{:S(2)}) copy-start(bf16[8,512,2,64]{1,0,3,2:T(8,128)(2,1)} %get-tuple-element.248) | copy-start | bytes 3145732
  454.9 95.0 %copy-start.5 = (bf16[8,512,2,64]{1,0,3,2:T(8,128)(2,1)S(1)}, bf16[8,512,2,64]{1,0,3,2:T(8,128)(2,1)}, u32[]{:S(2)}) copy-start(bf16[8,512,2,64]{1,0,3,2:T(8,128)(2,1)} %get-tuple-element.250) | copy-start | bytes 3145732
  661.7 2.8 copy-start.12
  661.7 76.7 %copy-start.6 = (bf16[4,8,2048]{2,1,0:T(8,128)(2,1)S(1)}, bf16[4,8,2048]{2,1,0:T(8,128)(2,1)}, u32[]{:S(2)}) copy-start(bf16[4,8,2048]{2,1,0:T(8,128)(2,1)} %param.22) | copy-start | bytes 393220
  738.4 2.5 copy-start.10
  738.4 3.1 copy-start.9
  741.0 1.1 copy-start.8
Sparse Core Ops, SparseCore 0:
  662.9 75.5 all-reduce.3
